TPU v7x, 256 devices: a whole 4x4x8 slice. The times are simulated.
256 devices in a mesh: row: 16 (over x_lo, z), col: 16 (over y, x_hi, core).
Axes of the slice: x: 4 (x_hi: 2, x_lo: 2; x = x_hi * 2 + x_lo), y: 4, z: 8, core: 2. Of those that a mesh axis runs over, the one named last changes fastest.
Arguments:
- queries: bfloat16 [65536, 2048], P(('row', 'col')), may hold values from -200 to 200
- keys: bfloat16 [65536, 512], P(('row', 'col')), may hold values from -6 to 6
- values: bfloat16 [65536, 512], P(('row', 'col')), may hold values from -6 to 6
- mid_key_weight: bfloat16 [1024, 128], replicated, may hold values from -0.1875 to 0.1875
- mid_value_weight: bfloat16 [1024, 128], replicated, may hold values from -0.1875 to 0.1875
- far_key_weight: bfloat16 [2048, 128], replicated, may hold values from -0.125 to 0.125
- far_value_weight: bfloat16 [2048, 128], replicated, may hold values from -0.125 to 0.125
Outputs:
- attended: bfloat16 [65536, 2048], P(('row', 'col'))
All inputs are finite; a program needn't handle non-finite values.
Results may differ from a plain program's by a relative error of at most 0.012.
Values may be sent and summed in bfloat16 or wider, within the bound.
No kernel may reach another device: no remote copies, remote signals or barrier semaphores. Data moves between devices by JAX's collectives and lax.ppermute only.
A program may use at most 128 MiB of HBM per device.

v0:
```python
import jax
import jax.numpy as jnp
from jax import lax
from jax.sharding import PartitionSpec as P

HQ = 16
HK = 4
DH = 128
BLOCK = 512
MID = 8
FAR = 16


NEG_FILL = -1e30


def from_behind(block, axis, distance):
    devices = range(lax.axis_size(axis))
    route = [(i - distance, i) for i in devices if i - distance in devices]
    return lax.ppermute(block, axis, route)


def laid_out(tiles, dim):
    lengths = list(tiles.shape[1:])
    lengths[dim] *= tiles.shape[0]
    return jnp.moveaxis(tiles, 0, dim).reshape(lengths)


def gather_packed(arrays, axis, dims):
    vector = jnp.concatenate([a.reshape(-1) for a in arrays])
    lines, at, finished = (lax.all_gather(vector, axis), 0, [])
    for a, dim in zip(arrays, dims):
        tiles = lines[:, at : at + a.size].reshape(-1, *a.shape)
        finished.append(laid_out(tiles, dim))
        at += a.size
    return tuple(finished)


def squeeze_groups(source, weight, squeeze):
    group_count = source.shape[0] // squeeze
    grouped = (
        source.reshape(group_count, squeeze, HK, DH)
        .transpose(0, 2, 1, 3)
        .reshape(group_count, HK, squeeze * DH)
    )
    merged = jnp.einsum("nhr,rd->nhd", grouped, weight, preferred_element_type=jnp.float32)
    return merged.astype(jnp.bfloat16).reshape(group_count, HK * DH)


def attend(queries, keys, values, visible):
    group_size = HQ // HK
    query_rows = queries.shape[0]
    query4 = queries.reshape(query_rows, HK, group_size, DH)
    key_heads = keys.reshape(keys.shape[0], HK, DH)
    value_heads = values.reshape(values.shape[0], HK, DH)
    scores = jnp.einsum(
        "thgd,shd->hgts", query4, key_heads, preferred_element_type=jnp.float32
    ) * DH ** (-0.5)
    top_score = jnp.max(jnp.where(visible, scores, NEG_FILL), axis=-1, keepdims=True)
    weights = jnp.exp(jnp.where(visible, scores - top_score, NEG_FILL))
    weight_sum = jnp.sum(weights, axis=-1)
    mixed_out = jnp.einsum(
        "hgts,shd->thgd",
        weights.astype(jnp.bfloat16),
        value_heads,
        preferred_element_type=jnp.float32,
    )
    weight_sum = jnp.transpose(weight_sum, (2, 0, 1))[..., None]
    return (mixed_out / jnp.maximum(weight_sum, 1.0)).reshape(query_rows, HQ * DH)


def body(queries, keys, values, mid_key_weight, mid_value_weight, far_key_weight, far_value_weight):
    tok_rows = queries.shape[0]
    columns = lax.axis_size("col")
    device_pos = lax.axis_index(("row", "col"))
    grid_row = device_pos // columns
    first_pos = device_pos * tok_rows
    query_pos = first_pos + jnp.arange(tok_rows, dtype=jnp.int32)
    near_pair = jnp.stack((keys, values))
    window = [near_pair]
    for offset in (1, 2, 3):
        window.insert(0, from_behind(near_pair, ("row", "col"), offset))
    near_all = jnp.concatenate(window, axis=1)
    key_pos = first_pos - 3 * tok_rows + jnp.arange(4 * tok_rows, dtype=jnp.int32)
    near_seen = (
        (key_pos[None, :] <= query_pos[:, None])
        & (key_pos[None, :] >= 0)
        & (key_pos[None, :] // BLOCK >= query_pos[:, None] // BLOCK - 1)
    )
    near_out = attend(queries, near_all[0], near_all[1], near_seen)
    mid_pair = jnp.stack(
        (squeeze_groups(keys, mid_key_weight, MID), squeeze_groups(values, mid_value_weight, MID))
    )
    far_pair = jnp.stack(
        (squeeze_groups(keys, far_key_weight, FAR), squeeze_groups(values, far_value_weight, FAR))
    )
    row_mid, row_far = gather_packed((mid_pair, far_pair), "col", (1, 1))
    all_far = lax.all_gather(row_far, "row", axis=1, tiled=True)
    mid_count = row_mid.shape[1]
    mid_end = (
        grid_row * (columns * tok_rows) + MID * jnp.arange(mid_count, dtype=jnp.int32) + MID - 1
    )
    mid_out = attend(queries, row_mid[0], row_mid[1], mid_end[None, :] <= query_pos[:, None])
    far_count = all_far.shape[1]
    far_row = jnp.arange(far_count, dtype=jnp.int32) // (columns * tok_rows // FAR)
    far_mask = far_row < grid_row
    block_rows = min(64, tok_rows)
    query_blocks = queries.reshape(tok_rows // block_rows, block_rows, queries.shape[1])

    def far_block(query_block):
        seen = jnp.broadcast_to(far_mask[None, :], (block_rows, far_count))
        return attend(query_block, all_far[0], all_far[1], seen)

    far_out = lax.map(far_block, query_blocks).reshape(tok_rows, queries.shape[1])
    return (near_out + mid_out + far_out).astype(jnp.bfloat16)


def solution(mesh):
    return jax.shard_map(
        body,
        mesh=mesh,
        in_specs=(
            P(("row", "col"), None),
            P(("row", "col"), None),
            P(("row", "col"), None),
            P(),
            P(),
            P(),
            P(),
        ),
        out_specs=P(("row", "col"), None),
        check_vma=False,
    )
```

profile of v0, /device:TPU:1, one launch (start us, length us, event | category | flops | bytes accessed | tf_op | source)
XLA Modules:
  0.0 347.9 jit_solution(6917983443919342149)
XLA Ops:
  12.2 55.6 %all-gather.6.cloned.1.call-done = bf16[786432]{0:T(1024)(128)(2,1)} async-done(((bf16[49152]{0:T(1024)(128)(2,1)}), bf16[786432]{0:T(1024)(128)(2,1)}) %all-gather.6.cloned.1.call-update) | async-done | bytes 1572880 | tf_op jit(solution)/shard_map/all_gather | solution.py:31
  71.9 3.8 %collective-permute-start = (bf16[2,256,512]{1,2,0:T(8,128)(2,1)}, bf16[2,256,512]{1,2,0:T(8,128)(2,1)}, u32[]{:S(2)}, u32[]{:S(2)}) collective-permute-start(bf16[2,256,512]{1,2,0:T(8,128)(2,1)} %pad_maximum_fusion), channel_id=1, source_target_pairs={{0,3},{1,4},{2,5},{3,6},{4,7},{5,8},{6,9},{7,10},{8,11},{9,12},{10... | collective-permute-start | bytes 1572872 | tf_op jit(solution)/shard_map/ppermute | solution.py:20
  77.9 4.6 %collective-permute-start.2 = (bf16[2,256,512]{1,2,0:T(8,128)(2,1)}, bf16[2,256,512]{1,2,0:T(8,128)(2,1)}, u32[]{:S(2)}, u32[]{:S(2)}) collective-permute-start(bf16[2,256,512]{1,2,0:T(8,128)(2,1)} %pad_maximum_fusion), channel_id=1, source_target_pairs={{0,1},{1,2},{2,3},{3,4},{4,5},{5,6},{6,7},{7,8},{8,9},{9,10},{10,1... | collective-permute-start | bytes 1572872 | tf_op jit(solution)/shard_map/ppermute | solution.py:20
  85.2 3.6 %collective-permute-done = bf16[2,256,512]{1,2,0:T(8,128)(2,1)} collective-permute-done((bf16[2,256,512]{1,2,0:T(8,128)(2,1)}, bf16[2,256,512]{1,2,0:T(8,128)(2,1)}, u32[]{:S(2)}, u32[]{:S(2)}) %collective-permute-start) | collective-permute-done | bytes 524320 | tf_op jit(solution)/shard_map/ppermute | solution.py:20
  88.9 84.5 %collective-permute-done.1 = bf16[2,256,512]{1,2,0:T(8,128)(2,1)} collective-permute-done((bf16[2,256,512]{1,2,0:T(8,128)(2,1)}, bf16[2,256,512]{1,2,0:T(8,128)(2,1)}, u32[]{:S(2)}, u32[]{:S(2)}) %collective-permute-start.1) | collective-permute-done | bytes 524320 | tf_op jit(solution)/shard_map/ppermute | solution.py:20
  173.4 8.8 %collective-permute-done.2 = bf16[2,256,512]{1,2,0:T(8,128)(2,1)} collective-permute-done((bf16[2,256,512]{1,2,0:T(8,128)(2,1)}, bf16[2,256,512]{1,2,0:T(8,128)(2,1)}, u32[]{:S(2)}, u32[]{:S(2)}) %collective-permute-start.2) | collective-permute-done | bytes 524320 | tf_op jit(solution)/shard_map/ppermute | solution.py:20
  185.2 11.3 %fusion.112 = (f32[4,4,256]{2,1,0:T(4,128)S(1)}, bf16[4,4,256,1024]{2,3,1,0:T(8,128)(2,1)}) fusion(pred[256,1024]{0,1:T(8,128)(4,1)S(1)} %compare_and_fusion, bf16[1024,4,128,1]{0,2,3,1:T(8,128)(2,1)} %bitcast.193, bf16[256,4,4,128]{3,2,1,0:T(4,128)(2,1)S(1)} %copy-done.6), kind=kOutput, calls=%fused_computation.117 | convolution fusion | flops 2176844800 | bytes 10764288 | tf_op jit(solution)/shard_map/sub | solution.py:60
  197.2 5.3 %fusion.103 = (f32[4,4,256]{2,1,0:T(4,128)S(1)}, bf16[4,4,256,512]{2,3,1,0:T(8,128)(2,1)}) fusion(pred[256,512]{0,1:T(8,128)(4,1)S(1)} %broadcast_compare_fusion, bf16[256,4,4,128]{3,2,1,0:T(4,128)(2,1)S(1)} %copy-done.6, bf16[512,4,128,1]{2,1,0,3:T(4,128)(2,1)S(1)} %bitcast.194), kind=kOutput, calls=%fused_computation.116 | convolution fusion | flops 1088422400 | bytes 5914624 | tf_op jit(solution)/shard_map/sub | solution.py:60
  202.5 3.1 fusion.48
  205.6 6.0 %fusion.56 = f32[256,4,4,128]{0,3,2,1:T(8,128)} fusion(f32[4,128,4,256]{3,1,2,0:T(8,128)S(1)} %fusion.48, bf16[1024,4,128,1]{0,2,3,1:T(8,128)(2,1)S(1)} %bitcast.192, bf16[4,4,256,1024]{2,3,1,0:T(8,128)(2,1)} %get-tuple-element.77, f32[256,4,4]{0,2,1:T(4,128)S(1)} %maximum_bitcast_fusion.1, f32[256,4,4]{0,2,1:T(4,128)S(1)} %maximum_bitcast_fusion.2), kind=kOutput, calls=%fused_computation.61 | convolution fusion | flops 1075314688 | bytes 13664256 | tf_op jit(solution)/shard_map/hgts,shd->thgd/dot_general | solution.py:62
  213.5 11.8 %copy.86 = bf16[2,4096,512]{1,2,0:T(8,128)(2,1)} copy(bf16[2,4096,512]{2,1,0:T(8,128)(2,1)} %all-gather.4.cloned.1.call-done) | data formatting | bytes 16777216
  225.4 112.9 %while.11 = (s32[]{:T(128)}, f32[4,64,2048]{2,1,0:T(8,128)}, bf16[4,64,2048]{2,1,0:T(8,128)(2,1)}, bf16[2,4096,512]{1,2,0:T(8,128)(2,1)}, s32[]{:T(128)}, /*index=5*/s32[]{:T(128)}) while((s32[]{:T(128)}, f32[4,64,2048]{2,1,0:T(8,128)}, bf16[4,64,2048]{2,1,0:T(8,128)(2,1)}, bf16[2,4096,512]{1,2,0:T(8,128)(2,1)}, s32[]{:T(128)}, ...), condition=%wide.region_7.8_spmd.clone, body=%wide.region_4.7_spmd.clone.sunk | while | flops 3250758656 | bytes 46948940 | solution.py:114
  226.5 6.0 %fusion.144 = (bf16[1,4096,512]{1,2,0:T(8,128)(2,1)}, bf16[1,4096,512]{1,2,0:T(8,128)(2,1)}) fusion(bf16[2,4096,512]{1,2,0:T(8,128)(2,1)} %get-tuple-element.142), kind=kLoop, calls=%fused_computation.112.clone.1 | loop fusion | bytes 16777216 | tf_op jit(solution)/shard_map/while/body/eval_jaxpr/slice | solution.py:112
  232.5 12.8 %fusion.146 = (f32[4,4,64]{2,1,0:T(4,128)S(1)}, bf16[4,4,64,4096]{3,2,1,0:T(8,128)(2,1)}) fusion(pred[4096]{0:T(1024)(128)(4,1)S(1)} %fusion.145, bf16[4096,4,128,1]{0,2,3,1:T(8,128)(2,1)} %bitcast.175, bf16[64,4,4,128]{3,2,1,0:T(4,128)(2,1)S(1)} %reshape.194), kind=kOutput, calls=%fused_computation.113.clone.1 | convolution fusion | flops 2176847872 | bytes 12853248 | tf_op jit(solution)/shard_map/while/body/eval_jaxpr/sub | solution.py:60
  245.3 6.9 %fusion.147 = f32[64,4,4,128]{3,0,2,1:T(8,128)S(1)} fusion(bf16[4096,4,128,1]{0,2,3,1:T(8,128)(2,1)} %bitcast.174, bf16[4,4,64,4096]{3,2,1,0:T(8,128)(2,1)} %get-tuple-element.125, f32[64,4,4]{0,2,1:T(4,128)S(1)} %maximum_bitcast_fusion.4), kind=kOutput, calls=%fused_computation.15.clone.1 | convolution fusion | flops 1073872896 | bytes 13111296 | tf_op jit(solution)/shard_map/while/body/eval_jaxpr/hgts,shd->thgd/dot_general | solution.py:62
  254.7 6.0 %fusion.144 = (bf16[1,4096,512]{1,2,0:T(8,128)(2,1)}, bf16[1,4096,512]{1,2,0:T(8,128)(2,1)}) fusion(bf16[2,4096,512]{1,2,0:T(8,128)(2,1)} %get-tuple-element.142), kind=kLoop, calls=%fused_computation.112.clone.1 | loop fusion | bytes 16777216 | tf_op jit(solution)/shard_map/while/body/eval_jaxpr/slice | solution.py:112
  260.7 12.8 %fusion.146 = (f32[4,4,64]{2,1,0:T(4,128)S(1)}, bf16[4,4,64,4096]{3,2,1,0:T(8,128)(2,1)}) fusion(pred[4096]{0:T(1024)(128)(4,1)S(1)} %fusion.145, bf16[4096,4,128,1]{0,2,3,1:T(8,128)(2,1)} %bitcast.175, bf16[64,4,4,128]{3,2,1,0:T(4,128)(2,1)S(1)} %reshape.194), kind=kOutput, calls=%fused_computation.113.clone.1 | convolution fusion | flops 2176847872 | bytes 12853248 | tf_op jit(solution)/shard_map/while/body/eval_jaxpr/sub | solution.py:60
  273.5 6.9 %fusion.147 = f32[64,4,4,128]{3,0,2,1:T(8,128)S(1)} fusion(bf16[4096,4,128,1]{0,2,3,1:T(8,128)(2,1)} %bitcast.174, bf16[4,4,64,4096]{3,2,1,0:T(8,128)(2,1)} %get-tuple-element.125, f32[64,4,4]{0,2,1:T(4,128)S(1)} %maximum_bitcast_fusion.4), kind=kOutput, calls=%fused_computation.15.clone.1 | convolution fusion | flops 1073872896 | bytes 13111296 | tf_op jit(solution)/shard_map/while/body/eval_jaxpr/hgts,shd->thgd/dot_general | solution.py:62
  283.0 6.0 %fusion.144 = (bf16[1,4096,512]{1,2,0:T(8,128)(2,1)}, bf16[1,4096,512]{1,2,0:T(8,128)(2,1)}) fusion(bf16[2,4096,512]{1,2,0:T(8,128)(2,1)} %get-tuple-element.142), kind=kLoop, calls=%fused_computation.112.clone.1 | loop fusion | bytes 16777216 | tf_op jit(solution)/shard_map/while/body/eval_jaxpr/slice | solution.py:112
  288.9 12.8 %fusion.146 = (f32[4,4,64]{2,1,0:T(4,128)S(1)}, bf16[4,4,64,4096]{3,2,1,0:T(8,128)(2,1)}) fusion(pred[4096]{0:T(1024)(128)(4,1)S(1)} %fusion.145, bf16[4096,4,128,1]{0,2,3,1:T(8,128)(2,1)} %bitcast.175, bf16[64,4,4,128]{3,2,1,0:T(4,128)(2,1)S(1)} %reshape.194), kind=kOutput, calls=%fused_computation.113.clone.1 | convolution fusion | flops 2176847872 | bytes 12853248 | tf_op jit(solution)/shard_map/while/body/eval_jaxpr/sub | solution.py:60
  301.7 6.9 %fusion.147 = f32[64,4,4,128]{3,0,2,1:T(8,128)S(1)} fusion(bf16[4096,4,128,1]{0,2,3,1:T(8,128)(2,1)} %bitcast.174, bf16[4,4,64,4096]{3,2,1,0:T(8,128)(2,1)} %get-tuple-element.125, f32[64,4,4]{0,2,1:T(4,128)S(1)} %maximum_bitcast_fusion.4), kind=kOutput, calls=%fused_computation.15.clone.1 | convolution fusion | flops 1073872896 | bytes 13111296 | tf_op jit(solution)/shard_map/while/body/eval_jaxpr/hgts,shd->thgd/dot_general | solution.py:62
  311.2 6.0 %fusion.144 = (bf16[1,4096,512]{1,2,0:T(8,128)(2,1)}, bf16[1,4096,512]{1,2,0:T(8,128)(2,1)}) fusion(bf16[2,4096,512]{1,2,0:T(8,128)(2,1)} %get-tuple-element.142), kind=kLoop, calls=%fused_computation.112.clone.1 | loop fusion | bytes 16777216 | tf_op jit(solution)/shard_map/while/body/eval_jaxpr/slice | solution.py:112
  317.1 12.8 %fusion.146 = (f32[4,4,64]{2,1,0:T(4,128)S(1)}, bf16[4,4,64,4096]{3,2,1,0:T(8,128)(2,1)}) fusion(pred[4096]{0:T(1024)(128)(4,1)S(1)} %fusion.145, bf16[4096,4,128,1]{0,2,3,1:T(8,128)(2,1)} %bitcast.175, bf16[64,4,4,128]{3,2,1,0:T(4,128)(2,1)S(1)} %reshape.194), kind=kOutput, calls=%fused_computation.113.clone.1 | convolution fusion | flops 2176847872 | bytes 12853248 | tf_op jit(solution)/shard_map/while/body/eval_jaxpr/sub | solution.py:60
  329.9 6.9 %fusion.147 = f32[64,4,4,128]{3,0,2,1:T(8,128)S(1)} fusion(bf16[4096,4,128,1]{0,2,3,1:T(8,128)(2,1)} %bitcast.174, bf16[4,4,64,4096]{3,2,1,0:T(8,128)(2,1)} %get-tuple-element.125, f32[64,4,4]{0,2,1:T(4,128)S(1)} %maximum_bitcast_fusion.4), kind=kOutput, calls=%fused_computation.15.clone.1 | convolution fusion | flops 1073872896 | bytes 13111296 | tf_op jit(solution)/shard_map/while/body/eval_jaxpr/hgts,shd->thgd/dot_general | solution.py:62
  (105 shorter events, 33.1 us)
Async XLA Ops:
  6.5 1.4 copy-start
  6.5 4.2 %copy-start.3 = (bf16[256,512]{1,0:T(8,128)(2,1)S(1)}, bf16[256,512]{1,0:T(8,128)(2,1)}, u32[]{:S(2)}) copy-start(bf16[256,512]{1,0:T(8,128)(2,1)} %param.10) | copy-start | bytes 786436
  6.5 4.5 %copy-start.4 = (bf16[256,512]{1,0:T(8,128)(2,1)S(1)}, bf16[256,512]{1,0:T(8,128)(2,1)}, u32[]{:S(2)}) copy-start(bf16[256,512]{1,0:T(8,128)(2,1)} %param.11) | copy-start | bytes 786436
  6.5 4.2 %copy-start.8 = (bf16[1024,128]{1,0:T(8,128)(2,1)S(1)}, bf16[1024,128]{1,0:T(8,128)(2,1)}, u32[]{:S(2)}) copy-start(bf16[1024,128]{1,0:T(8,128)(2,1)} %param.12) | copy-start | bytes 786436
  6.5 4.6 %copy-start.9 = (bf16[1024,128]{1,0:T(8,128)(2,1)S(1)}, bf16[1024,128]{1,0:T(8,128)(2,1)}, u32[]{:S(2)}) copy-start(bf16[1024,128]{1,0:T(8,128)(2,1)} %param.13) | copy-start | bytes 786436
  6.5 61.3 %all-gather.6.cloned.1.call-start = ((), (), s32[]{:S(2)}) async-start(), calls=%async_computation.1 | async-start | bytes 1671168 | tf_op jit(solution)/shard_map/all_gather | solution.py:31
  11.2 59.7 %copy-start.5 = (bf16[256,512]{1,0:T(8,128)(2,1)S(1)}, bf16[256,512]{1,0:T(8,128)(2,1)}, u32[]{:S(2)}) copy-start(bf16[256,512]{1,0:T(8,128)(2,1)} %param.11) | copy-start | bytes 786436
  12.2 70.4 %copy-start.2 = (bf16[256,2048]{1,0:T(8,128)(2,1)S(1)}, bf16[256,2048]{1,0:T(8,128)(2,1)}, u32[]{:S(2)}) copy-start(bf16[256,2048]{1,0:T(8,128)(2,1)} %param.9) | copy-start | bytes 3145732
  12.2 201.4 %all-gather.4.cloned.1.call-start = ((), (), s32[]{:S(2)}) async-start(), calls=%async_computation | async-start | bytes 8912896 | tf_op jit(solution)/shard_map/all_gather | solution.py:98
  71.9 17.0 %collective-permute-start = (bf16[2,256,512]{1,2,0:T(8,128)(2,1)}, bf16[2,256,512]{1,2,0:T(8,128)(2,1)}, u32[]{:S(2)}, u32[]{:S(2)}) collective-permute-start(bf16[2,256,512]{1,2,0:T(8,128)(2,1)} %pad_maximum_fusion), channel_id=1, source_target_pairs={{0,3},{1,4},{2,5},{3,6},{4,7},{5,8},{6,9},{7,10},{8,11},{9,12},{10... | collective-permute-start | bytes 1572872 | tf_op jit(solution)/shard_map/ppermute | solution.py:20
  75.7 97.7 %collective-permute-start.1 = (bf16[2,256,512]{1,2,0:T(8,128)(2,1)}, bf16[2,256,512]{1,2,0:T(8,128)(2,1)}, u32[]{:S(2)}, u32[]{:S(2)}) collective-permute-start(bf16[2,256,512]{1,2,0:T(8,128)(2,1)} %pad_maximum_fusion), channel_id=1, source_target_pairs={{0,2},{1,3},{2,4},{3,5},{4,6},{5,7},{6,8},{7,9},{8,10},{9,11},{10,... | collective-permute-start | bytes 1572872 | tf_op jit(solution)/shard_map/ppermute | solution.py:20
  77.9 104.3 %collective-permute-start.2 = (bf16[2,256,512]{1,2,0:T(8,128)(2,1)}, bf16[2,256,512]{1,2,0:T(8,128)(2,1)}, u32[]{:S(2)}, u32[]{:S(2)}) collective-permute-start(bf16[2,256,512]{1,2,0:T(8,128)(2,1)} %pad_maximum_fusion), channel_id=1, source_target_pairs={{0,1},{1,2},{2,3},{3,4},{4,5},{5,6},{6,7},{7,8},{8,9},{9,10},{10,1... | collective-permute-start | bytes 1572872 | tf_op jit(solution)/shard_map/ppermute | solution.py:20
  85.2 99.9 %copy-start.6 = (bf16[256,4,4,128]{3,2,1,0:T(4,128)(2,1)S(1)}, bf16[256,4,4,128]{3,2,1,0:T(4,128)(2,1)}, u32[]{:S(2)}) copy-start(bf16[256,4,4,128]{3,2,1,0:T(4,128)(2,1)} %reshape.163) | copy-start | bytes 3145732
  202.5 3.1 copy-start.7
  338.2 2.9 copy-start.1
Sparse Core Ops, SparseCore 0:
  12.3 55.5 all-gather.5
  70.9 99.4 all-gather.3
where the time goes:
time: 354 us; the launch traced here: 348 us
  waiting for transfers between devices  153 us (43%)
  matrix products  106 us (30%)
  local copies, waits for them, and re-layouts  57.4 us (16%)
  between operations  13.8 us (4%)
  starting transfers between devices  10.7 us (3%)
  other arithmetic  7.01 us (2%)
    ppermute x3, waiting for transfers between devices, from_behind(): return lax.ppermute(block, axis, route)  97 us
    sub x6, matrix products, attend(): weights = jnp.exp(jnp.where(visible, scores - top_score, NEG_FILL))  67.6 us
    all_gather x1, waiting for transfers between devices, gather_packed(): lines, at, finished = (lax.all_gather(vector, axis), 0, [])  55.6 us
    dot_general x6, matrix products, attend(): jnp.einsum('hgts,shd->thgd', weights.astype(jnp.bfloat16), value_heads, p...  36.7 us
    slice x4, local copies, waits for them, and re-layouts, far_block(): return attend(query_block, all_far[0], all_far[1], seen)  23.8 us
    unnamed x27, local copies, waits for them, and re-layouts  12.6 us
    ppermute x3, starting transfers between devices, from_behind(): return lax.ppermute(block, axis, route)  10.6 us
  transfers between devices with their start and end apart: 5, of which 4 were waited for; matrix products, arithmetic and copies ran while one was open for 10% of the time, Pallas kernels for 0%

commit v1 on v0

v1 whole, which is shorter than its diff:
```python
import functools

import jax
import jax.numpy as jnp
import numpy as np
from jax import lax
from jax.experimental import pallas as pl
from jax.experimental.pallas import tpu as pltpu
from jax.sharding import PartitionSpec as P

HQ = 16
HK = 4
DH = 128
BLOCK = 512
MID = 8
FAR = 16
TOK = 256
CHIP = 2 * TOK
HEADS = HQ // 2
NEG = -1e30
EXP2_SCALE = float(DH**-0.5 * np.log2(np.e))
BF16 = jnp.bfloat16
F32 = jnp.float32
NT = (((1,), (1,)), ((), ()))
N_X, N_Y, N_Z = 4, 4, 8
AXES = ("row", "col")


def place(d):
    row, col = d // 16, d % 16
    return (col // 2 % 2) * 2 + row // N_Z, col // 4, row % N_Z, col % 2


def device(x, y, z, core):
    return ((x % 2) * N_Z + z) * 16 + (y * 2 + x // 2) * 2 + core


def shift(v, axis, by, wrap=True, from_even=False):
    pairs = []
    for d in range(256):
        at = list(place(d))
        if from_even and at[0] % 2:
            continue
        size = (N_X, N_Y, N_Z)[axis]
        to = at[axis] + by
        if not wrap and not 0 <= to < size:
            continue
        at[axis] = to % size
        pairs.append((d, device(*at)))
    return lax.ppermute(v, AXES, pairs)


def other_core(v):
    return lax.ppermute(v, AXES, [(d, d ^ 1) for d in range(256)])


def next_chip(v):
    return lax.ppermute(v, AXES, [(d, d + 2) for d in range(254)])


def squeeze_kernel(s_ref, k_ref, v_ref, got_ref, mk_ref, mv_ref, fk_ref, fv_ref, chip_ref, mid_ref, far_ref, x_ref):
    core = s_ref[0]
    for i, (own_ref, m_ref, f_ref) in enumerate(((k_ref, mk_ref, fk_ref), (v_ref, mv_ref, fv_ref))):
        for h in range(2):
            lanes = slice(h * DH, (h + 1) * DH)
            own = own_ref[:, lanes].astype(F32)
            got = got_ref[i, :, lanes].astype(F32)
            x_ref[pl.ds(pl.multiple_of(h * CHIP + core * TOK, TOK), TOK), :] = own
            x_ref[pl.ds(pl.multiple_of(h * CHIP + (1 - core) * TOK, TOK), TOK), :] = got
            chip_ref[i, :, lanes] = x_ref[h * CHIP : (h + 1) * CHIP, :].astype(BF16)
        for run, w_ref in ((MID, m_ref), (FAR, f_ref)):
            rows = 2 * CHIP // run
            laid = jnp.concatenate(
                [x_ref[pl.ds(j, rows, stride=run), :].astype(BF16) for j in range(run)], axis=1
            )
            merged = jnp.dot(laid, w_ref[...], preferred_element_type=F32).astype(BF16)
            half = rows // 2
            for h in range(2):
                part = merged[h * half : (h + 1) * half]
                if run == MID:
                    mid_ref[0, i, :, h * DH : (h + 1) * DH] = part
                else:
                    far_ref[h, 0, i] = part


def squeeze(scalars, k_own, v_own, got, mk, mv, fk, fv):
    whole = lambda shape: pl.BlockSpec(shape, lambda i, s: (0,) * len(shape))
    return pl.pallas_call(
        squeeze_kernel,
        grid_spec=pltpu.PrefetchScalarGridSpec(
            num_scalar_prefetch=1,
            grid=(1,),
            in_specs=[
                pl.BlockSpec((TOK, 2 * DH), lambda i, s: (0, s[0])),
                pl.BlockSpec((TOK, 2 * DH), lambda i, s: (0, s[0])),
                whole((2, TOK, 2 * DH)),
                whole((MID * DH, DH)),
                whole((MID * DH, DH)),
                whole((FAR * DH, DH)),
                whole((FAR * DH, DH)),
            ],
            out_specs=[
                whole((2, CHIP, 2 * DH)),
                whole((1, 2, CHIP // MID, 2 * DH)),
                whole((2, 1, 2, CHIP // FAR, DH)),
            ],
            scratch_shapes=[pltpu.VMEM((2 * CHIP, DH), F32)],
        ),
        out_shape=[
            jax.ShapeDtypeStruct((2, CHIP, 2 * DH), BF16),
            jax.ShapeDtypeStruct((1, 2, CHIP // MID, 2 * DH), BF16),
            jax.ShapeDtypeStruct((2, 1, 2, CHIP // FAR, DH), BF16),
        ],
        name="squeeze",
        compiler_params=pltpu.CompilerParams(vmem_limit_bytes=16 << 20),
        cost_estimate=pl.CostEstimate(flops=4 * 10**8, bytes_accessed=3 << 20, transcendentals=0),
    )(scalars, k_own, v_own, got, mk, mv, fk, fv)


def step(q, k, v, fix, state):
    s = lax.dot_general(q, k, NT, preferred_element_type=F32)
    if fix is not None:
        s = fix(s)
    top = jnp.max(s, axis=1, keepdims=True)
    if state is not None:
        top = jnp.maximum(top, state[0])
    p = jnp.exp2((s - top) * EXP2_SCALE).astype(BF16)
    v = jnp.concatenate([v, jnp.ones(v.shape, BF16)], axis=1)
    got = jnp.dot(p, v, preferred_element_type=F32)
    if state is not None:
        got = got + state[1] * jnp.exp2((state[0] - top) * EXP2_SCALE)
    return top, got


def load_state(o_ref, stat_ref, t, h):
    stat = stat_ref[t]
    lane = lax.broadcasted_iota(jnp.int32, stat.shape, 1)
    top = jnp.sum(jnp.where(lane == h, stat, 0.0), axis=1, keepdims=True)
    total = jnp.sum(jnp.where(lane == HEADS + h, stat, 0.0), axis=1, keepdims=True)
    return top, jnp.concatenate([o_ref[t], jnp.broadcast_to(total, stat.shape)], axis=1)


def save_state(o_ref, stat_ref, t, h, state):
    top, got = state
    o_ref[t] = got[:, :DH]
    lane = lax.broadcasted_iota(jnp.int32, (TOK, DH), 1)
    old = jnp.where(h == 0, 0.0, stat_ref[t])
    stat_ref[t] = jnp.where(lane == h, top, jnp.where(lane == HEADS + h, got[:, DH:], old))


def finish(state):
    top, got = state
    return jnp.where(top > 0.5 * NEG, got[:, :DH] / jnp.maximum(got[:, DH:], 1.0), 0.0)


def own_kernel(s_ref, qa_ref, qb_ref, kv_ref, o_ref, stat_ref):
    h = pl.program_id(0)
    core = s_ref[0]
    for t, q_ref in enumerate((qa_ref, qb_ref)):
        base = core * TOK if t == 0 else (1 - core) * TOK
        q, state = q_ref[...], None
        for c in range(2):
            keys = slice(c * TOK, (c + 1) * TOK)

            def causal(s, c=c):
                row = lax.broadcasted_iota(jnp.int32, s.shape, 0) + base
                col = lax.broadcasted_iota(jnp.int32, s.shape, 1) + c * TOK
                return jnp.where(col <= row, s, NEG)

            state = step(q, kv_ref[0, keys], kv_ref[1, keys], causal, state)
        save_state(o_ref, stat_ref, t, h, state)


def near_mid_kernel(s_ref, qa_ref, qb_ref, kv_ref, m0_ref, m1_ref, m2_ref, m3_ref, tab_ref, o_in, stat_in, out_ref):
    h = pl.program_id(0)
    core = s_ref[0]
    hidden = jnp.where(s_ref[1] > 0, 0.0, NEG)
    mids = (m0_ref, m1_ref, m2_ref, m3_ref)
    mid_k = jnp.concatenate([m[:, 0].reshape(-1, DH) for m in mids], axis=0)
    mid_v = jnp.concatenate([m[:, 1].reshape(-1, DH) for m in mids], axis=0)
    ends = tab_ref[3:4, : mid_k.shape[0]]
    for t, q_ref in enumerate((qa_ref, qb_ref)):
        base = core * TOK if t == 0 else (1 - core) * TOK
        q = q_ref[...]
        near = step(q, kv_ref[0], kv_ref[1], lambda s: s + hidden, load_state(o_in, stat_in, t, h))

        def ended(s):
            row = lax.broadcasted_iota(jnp.int32, s.shape, 0) + base
            return jnp.where(ends <= row.astype(F32), s, NEG)

        mid = step(q, mid_k, mid_v, ended, None)
        out_ref[t] = finish(near) + finish(mid)


def far_kernel(parts, first, last, *refs):
    s_ref, qa_ref, qb_ref = refs[:3]
    part_refs, refs = refs[3 : 3 + 2 * len(parts)], refs[3 + 2 * len(parts) :]
    tab_ref, refs = refs[0], refs[1:]
    if not first:
        o_in, stat_in, refs = refs[0], refs[1], refs[2:]
    if last:
        sum_ref, keep_ref, send_ref = refs
    else:
        o_ref, stat_ref = refs
    h = pl.program_id(0)

    def run(half):
        for t, q_ref in enumerate((qa_ref, qb_ref)):
            q = q_ref[...]
            state = None if first else load_state(o_in, stat_in, t, h)
            for i, rows in enumerate(parts):
                ref = part_refs[2 * i + half]
                n = ref.shape[0] // 2
                for c in range(2):
                    pieces = slice(c * n, (c + 1) * n)
                    k = ref[pieces, 0].reshape(-1, DH)
                    v = ref[pieces, 1].reshape(-1, DH)
                    width = k.shape[0]
                    bias = tab_ref[rows[half] : rows[half] + 1, c * width : (c + 1) * width]
                    state = step(q, k, v, lambda s, bias=bias: s + bias, state)
            if last:
                (keep_ref, send_ref)[t][...] = (finish(state) + sum_ref[t]).astype(BF16)
            else:
                save_state(o_ref, stat_ref, t, h, state)

    @pl.when(h < HEADS // 2)
    def _():
        run(0)

    @pl.when(h >= HEADS // 2)
    def _():
        run(1)


Q_SPECS = [
    pl.BlockSpec((TOK, DH), lambda h, s: (0, s[0] * HEADS + h)),
    pl.BlockSpec((TOK, DH), lambda h, s: (0, h)),
]
KV_SPEC = pl.BlockSpec((2, CHIP, DH), lambda h, s: (0, 0, h // 2 // 2))
MID_SPEC = pl.BlockSpec((2, 2, CHIP // MID, DH), lambda h, s: (0, 0, 0, h // 4))
O_SPEC = pl.BlockSpec((2, TOK, DH), lambda h, s: (0, 0, h))
STAT_SPEC = pl.BlockSpec((2, TOK, DH), lambda h, s: (0, 0, 0))
TAB_SPEC = pl.BlockSpec((8, 1024), lambda h, s: (0, 0))
HALF_SPEC = pl.BlockSpec((TOK, DH), lambda h, s: (0, h))
O_SHAPE = jax.ShapeDtypeStruct((2, TOK, HEADS * DH), F32)
STAT_SHAPE = jax.ShapeDtypeStruct((2, TOK, DH), F32)
HALF_SHAPE = jax.ShapeDtypeStruct((TOK, HEADS * DH), BF16)


def call(kernel, name, keys, in_specs, out_specs, out_shape, *args):
    rows = CHIP * HEADS
    return pl.pallas_call(
        kernel,
        grid_spec=pltpu.PrefetchScalarGridSpec(
            num_scalar_prefetch=1, grid=(HEADS,), in_specs=in_specs, out_specs=out_specs
        ),
        out_shape=out_shape,
        name=name,
        compiler_params=pltpu.CompilerParams(vmem_limit_bytes=24 << 20),
        cost_estimate=pl.CostEstimate(
            flops=6 * rows * keys * DH, bytes_accessed=6 << 20, transcendentals=rows * keys
        ),
    )(*args)


def far_call(name, parts, chunks, scalars, qa, qb, tab, state=None, total=None):
    in_specs = list(Q_SPECS)
    args = [scalars, qa, qb]
    for a, b in chunks:
        for v in (a, b):
            in_specs.append(pl.BlockSpec(v.shape, lambda h, s: (0, 0, 0, 0)))
            args.append(v)
    in_specs.append(TAB_SPEC)
    args.append(tab)
    if state is not None:
        in_specs += [O_SPEC, STAT_SPEC]
        args += list(state)
    if total is not None:
        in_specs.append(O_SPEC)
        args.append(total)
        outs = [HALF_SPEC, HALF_SPEC], [HALF_SHAPE, HALF_SHAPE]
    else:
        outs = [O_SPEC, STAT_SPEC], [O_SHAPE, STAT_SHAPE]
    kernel = functools.partial(far_kernel, parts, state is None, total is not None)
    return call(kernel, name, 1024 * len(parts), in_specs, *outs, *args)


def tables(row, x, z, chip_row):
    z_at = np.array([0, 4, -1, 3, 1, 5, -2, 2])
    piece_z = jnp.asarray(np.tile(np.repeat(z_at, CHIP // FAR), 4), jnp.int32)
    piece_x = jnp.asarray(np.repeat(np.array([0, -1, 1, -2]), 8 * CHIP // FAR), jnp.int32)
    src_z = (z + piece_z) % N_Z
    rows_a = ((x + piece_x) % 2) * N_Z + src_z
    rows_same = (x % 2) * N_Z + src_z
    rows_other = ((x + 1) % 2) * N_Z + src_z
    bias = jnp.where(jnp.stack([rows_a, rows_same, rows_other]) < row, 0.0, NEG).astype(F32)
    y, x_hi = chip_row // 2, chip_row % 2
    back = jnp.asarray(np.repeat(np.arange(4), 128), jnp.int32)
    flip = jnp.asarray(np.tile(np.repeat(np.arange(2), 64), 4), jnp.int32)
    run = jnp.asarray(np.tile(np.arange(64), 8), jnp.int32)
    src = (y - back) * 2 + jnp.where(flip == 1, 1 - x_hi, x_hi)
    ends = ((src - chip_row) * CHIP + run * MID + MID - 1).astype(F32)
    ends = jnp.where(back > y, 1e9, ends)
    ends = jnp.concatenate([ends, jnp.full((512,), 1e9, F32)])
    return jnp.concatenate([bias, ends[None], jnp.zeros((4, 1024), F32)])


def body(queries, keys, values, mk, mv, fk, fv):
    row, col = lax.axis_index("row"), lax.axis_index("col")
    core, chip_row = col % 2, col // 2
    x, z = (chip_row % 2) * 2 + row // N_Z, row % N_Z
    scalars = jnp.stack([core, row * 8 + chip_row]).astype(jnp.int32)
    tab = tables(row, x, z, chip_row)

    def for_other(a):
        half = a.shape[1] // 2
        return jnp.where(core == 0, a[:, half:], a[:, :half])

    got = other_core(jnp.stack([for_other(keys), for_other(values)]))
    q_got = other_core(for_other(queries))
    chip_kv, mid, far = squeeze(scalars, keys, values, got, mk, mv, fk, fv)

    far = jnp.concatenate([far, shift(far, 2, 4)], axis=1)
    far = jnp.concatenate([far, shift(far, 2, 1), shift(far, 2, -1), shift(far, 2, 2)], axis=1)
    prev_kv = next_chip(chip_kv)
    mid = jnp.concatenate([mid, shift(mid, 0, 2)], axis=0)
    mids = [mid] + [shift(mid, 1, d, wrap=False) for d in (1, 2, 3)]
    a, b = far[0], far[1]
    a = jnp.concatenate(
        [a, shift(a, 0, 1, from_even=True), shift(a, 0, -1, from_even=True), shift(a, 0, 2)], axis=0
    )
    b = jnp.concatenate([b, shift(b, 1, 1), shift(b, 1, -1), shift(b, 1, 2)], axis=0)
    a1, b1 = shift(a, 1, 1), shift(b, 0, 1, from_even=True)
    a2, b2 = shift(a, 1, -1), shift(b, 0, -1, from_even=True)
    a3, b3 = shift(a, 1, 2), shift(b, 0, 2)

    near = call(
        own_kernel, "near_own", 512, Q_SPECS + [KV_SPEC], [O_SPEC, STAT_SPEC], [O_SHAPE, STAT_SHAPE],
        scalars, queries, q_got, chip_kv,
    )
    total = call(
        near_mid_kernel, "near_mid", 1024,
        Q_SPECS + [KV_SPEC] + [MID_SPEC] * 4 + [TAB_SPEC, O_SPEC, STAT_SPEC], O_SPEC, O_SHAPE,
        scalars, queries, q_got, prev_kv, *mids, tab, *near,
    )
    state = far_call("far_0", [(0, 1)], [(a, b)], scalars, queries, q_got, tab)
    state = far_call("far_1", [(0, 2), (0, 2)], [(a1, b1), (a2, b2)], scalars, queries, q_got, tab, state)
    keep, send = far_call("far_2", [(0, 1)], [(a3, b3)], scalars, queries, q_got, tab, state, total)
    back = other_core(send)
    return jnp.concatenate([jnp.where(core == 0, keep, back), jnp.where(core == 0, back, keep)], axis=1)


def solution(mesh):
    split = P(("row", "col"), None)
    return jax.shard_map(
        body,
        mesh=mesh,
        in_specs=(split, split, split, P(), P(), P(), P()),
        out_specs=split,
        check_vma=False,
    )
```

time: 354 us -> 131 us (0.37); the launches traced: 348 us -> 131 us
  waiting for transfers between devices: 153 us -> 10.5 us
  matrix products: 106 us -> 0 us
  local copies, waits for them, and re-layouts: 57.4 us -> 0.24 us
  Pallas kernels: 0 us -> 52.9 us
  starting transfers between devices: 10.7 us -> 62.3 us
  between operations: 13.8 us -> 0.46 us
    ppermute x3 -> x24, waiting for transfers between devices: 97 us -> 10.5 us  [the longest x20 7.45 us: shift(): return lax.ppermute(v, AXES, pairs)]
    sub x6 -> x0, matrix products: 67.6 us -> none  [attend(): weights = jnp.exp(jnp.where(visible, scores - top_score, NEG_FILL))]
    all_gather x2 -> x0, waiting for transfers between devices: 55.6 us -> none  [the longest x1 55.6 us: gather_packed(): lines, at, finished = (lax.all_gather(vector, axis), 0, [])]
    pallas_call x0 -> x6, Pallas kernels: none -> 52.9 us  [the longest x5 51.5 us: call(): pl.pallas_call(kernel, grid_spec=pltpu.PrefetchScalarGridSpec(num_scalar_...]
    ppermute x3 -> x24, starting transfers between devices: 10.6 us -> 62.3 us  [the longest x20 39.4 us: shift(): return lax.ppermute(v, AXES, pairs)]
    dot_general x10 -> x0, matrix products: 38.6 us -> none  [the longest x6 36.7 us: attend(): jnp.einsum('hgts,shd->thgd', weights.astype(jnp.bfloat16), value_heads, p...]
    slice x8 -> x0, local copies, waits for them, and re-layouts: 25.5 us -> none  [the longest x4 23.8 us: far_block(): return attend(query_block, all_far[0], all_far[1], seen)]
    unnamed x27 -> x30, local copies, waits for them, and re-layouts: 12.6 us -> 0.11 us
  transfers between devices with their start and end apart: 5 -> 24, of which waited for: 4 -> 5; matrix products, arithmetic and copies ran while one was open for 10% -> 2% of each run, Pallas kernels for 0% -> 33%
where the time goes in v1:
time: 131 us
  starting transfers between devices  62.3 us (48%)
  Pallas kernels  52.9 us (40%)
  waiting for transfers between devices  10.5 us (8%)
  other arithmetic  4.72 us (4%)
    pallas_call x5, Pallas kernels, call(): pl.pallas_call(kernel, grid_spec=pltpu.PrefetchScalarGridSpec(num_scalar_...  51.5 us
    ppermute x20, starting transfers between devices, shift(): return lax.ppermute(v, AXES, pairs)  39.4 us
    ppermute x3, starting transfers between devices, other_core(): return lax.ppermute(v, AXES, [(d, d ^ 1) for d in range(256)])  19.7 us
    ppermute x20, waiting for transfers between devices, shift(): return lax.ppermute(v, AXES, pairs)  7.45 us
    ppermute x1, starting transfers between devices, next_chip(): return lax.ppermute(v, AXES, [(d, d + 2) for d in range(254)])  3.11 us
    ppermute x3, waiting for transfers between devices, other_core(): return lax.ppermute(v, AXES, [(d, d ^ 1) for d in range(256)])  3.03 us
  transfers between devices with their start and end apart: 24, of which 5 were waited for; matrix products, arithmetic and copies ran while one was open for 2% of the time, Pallas kernels for 33%

profile of v1, /device:TPU:1, one launch (start us, length us, event | category | flops | bytes accessed | tf_op | source)
XLA Modules:
  0.0 131.1 jit_solution(8982526040734950813)
XLA Ops:
  0.1 1.4 %slice_select_fusion = bf16[256,1024]{1,0:T(8,128)(2,1)S(1)} fusion(bf16[256,2048]{1,0:T(8,128)(2,1)} %refs_1_.5, pred[]{:T(512)S(6)} %eq.20), kind=kLoop, calls=%fused_computation.3 | loop fusion | flops 262144 | bytes 1572865 | tf_op jit(solution)/shard_map/jit(_where)/select_n | solution.py:317
  1.5 3.3 %collective-permute-start = (bf16[256,1024]{1,0:T(8,128)(2,1)S(1)}, bf16[256,1024]{1,0:T(8,128)(2,1)S(1)}, u32[]{:S(2)}, u32[]{:S(2)}) collective-permute-start(bf16[256,1024]{1,0:T(8,128)(2,1)S(1)} %slice_select_fusion), channel_id=1, source_target_pairs={{0,1},{1,0},{2,3},{3,2},{4,5},{5,4},{6,7},{7,6},{8,9},{9,8},{10,11... | collective-permute-start | bytes 1572872 | tf_op jit(solution)/shard_map/ppermute | solution.py:54
  7.0 1.5 %collective-permute-done.1.got_ref = bf16[2,256,256]{2,1,0:T(8,128)(2,1)S(1)} collective-permute-done((bf16[2,256,256]{2,1,0:T(8,128)(2,1)}, bf16[2,256,256]{2,1,0:T(8,128)(2,1)S(1)}, u32[]{:S(2)}, u32[]{:S(2)}) %collective-permute-start.1) | collective-permute-done | bytes 262176 | tf_op jit(solution)/shard_map/ppermute | solution.py:54
  9.9 5.3 %collective-permute-start.2 = (bf16[2,1,2,32,128]{4,3,2,1,0:T(8,128)(2,1)S(1)}, bf16[2,1,2,32,128]{4,3,2,1,0:T(8,128)(2,1)S(1)}, u32[]{:S(2)}, u32[]{:S(2)}) collective-permute-start(bf16[2,1,2,32,128]{4,3,2,1,0:T(8,128)(2,1)S(1)} %get-tuple-element.16), channel_id=1, source_target_pairs={{0,64},{1,65},{2,66},{3,67},{4,68},{5,69},{6,70},{7,71},{8,72},{9,... | collective-permute-start | bytes 98312 | tf_op jit(solution)/shard_map/ppermute | solution.py:50
  15.2 1.6 %collective-permute-done.2 = bf16[2,1,2,32,128]{4,3,2,1,0:T(8,128)(2,1)S(1)} collective-permute-done((bf16[2,1,2,32,128]{4,3,2,1,0:T(8,128)(2,1)S(1)}, bf16[2,1,2,32,128]{4,3,2,1,0:T(8,128)(2,1)S(1)}, u32[]{:S(2)}, u32[]{:S(2)}) %collective-permute-start.2) | collective-permute-done | bytes 32800 | tf_op jit(solution)/shard_map/ppermute | solution.py:50
  17.7 2.8 %collective-permute-start.19 = (bf16[1,2,64,256]{3,2,1,0:T(8,128)(2,1)S(1)}, bf16[1,2,64,256]{3,2,1,0:T(8,128)(2,1)S(1)}, u32[]{:S(2)}, u32[]{:S(2)}) collective-permute-start(bf16[1,2,64,256]{3,2,1,0:T(8,128)(2,1)S(1)} %get-tuple-element.22), channel_id=1, source_target_pairs={{0,2},{1,3},{2,0},{3,1},{4,6},{5,7},{6,4},{7,5},{8,10},{9,11},{10,... | collective-permute-start | bytes 196616 | tf_op jit(solution)/shard_map/ppermute | solution.py:50
  20.5 3.0 %collective-permute-start.4 = (bf16[2,2,2,32,128]{4,3,2,1,0:T(8,128)(2,1)S(1)}, bf16[2,2,2,32,128]{4,3,2,1,0:T(8,128)(2,1)S(1)}, u32[]{:S(2)}, u32[]{:S(2)}) collective-permute-start(bf16[2,2,2,32,128]{4,3,2,1,0:T(8,128)(2,1)S(1)} %get-tuple-element.31), channel_id=1, source_target_pairs={{0,112},{1,113},{2,114},{3,115},{4,116},{5,117},{6,118},{7,119},{8... | collective-permute-start | bytes 196616 | tf_op jit(solution)/shard_map/ppermute | solution.py:50
  24.9 4.5 %collective-permute-done.5 = bf16[2,2,2,32,128]{4,3,2,1,0:T(8,128)(2,1)S(1)} collective-permute-done((bf16[2,2,2,32,128]{4,3,2,1,0:T(8,128)(2,1)S(1)}, bf16[2,2,2,32,128]{4,3,2,1,0:T(8,128)(2,1)S(1)}, u32[]{:S(2)}, u32[]{:S(2)}) %collective-permute-start.5) | collective-permute-done | bytes 65568 | tf_op jit(solution)/shard_map/ppermute | solution.py:50
  29.5 4.6 %collective-permute-start.7 = (bf16[8,2,32,128]{3,2,1,0:T(8,128)(2,1)S(1)}, bf16[8,2,32,128]{3,2,1,0:T(8,128)(2,1)S(1)}, u32[]{:S(2)}, u32[]{:S(2)}) collective-permute-start(bf16[8,2,32,128]{3,2,1,0:T(8,128)(2,1)S(1)} %get-tuple-element.30), channel_id=1, source_target_pairs={{0,130},{1,131},{2,128},{3,129},{4,134},{5,135},{6,132},{7,133},{8... | collective-permute-start | bytes 393224 | tf_op jit(solution)/shard_map/ppermute | solution.py:50
  35.5 3.0 %collective-permute-start.12 = (bf16[8,2,32,128]{3,2,1,0:T(8,128)(2,1)S(1)}, bf16[8,2,32,128]{3,2,1,0:T(8,128)(2,1)S(1)}, u32[]{:S(2)}, u32[]{:S(2)}) collective-permute-start(bf16[8,2,32,128]{3,2,1,0:T(8,128)(2,1)S(1)} %get-tuple-element.29), channel_id=1, source_target_pairs={{0,8},{1,9},{2,10},{3,11},{4,12},{5,13},{6,14},{7,15},{8,0},{9,1},... | collective-permute-start | bytes 393224 | tf_op jit(solution)/shard_map/ppermute | solution.py:50
  40.1 2.3 %collective-permute-start.20 = (bf16[2,2,64,256]{3,2,1,0:T(8,128)(2,1)S(1)}, bf16[2,2,64,256]{3,2,1,0:T(8,128)(2,1)S(1)}, u32[]{:S(2)}, u32[]{:S(2)}) collective-permute-start(bf16[2,2,64,256]{3,2,1,0:T(8,128)(2,1)S(1)} %constant_dynamic-update-slice_fusion.7.m0_ref), channel_id=1, source_target_pairs={{0,4},{1,5},{2,6},{3,7},{4,8},{5,9},{6,10},{7,11},{8,12},{9,13},{1... | collective-permute-start | bytes 393224 | tf_op jit(solution)/shard_map/ppermute | solution.py:50
  42.4 4.7 %collective-permute-start.21 = (bf16[2,2,64,256]{3,2,1,0:T(8,128)(2,1)S(1)}, bf16[2,2,64,256]{3,2,1,0:T(8,128)(2,1)S(1)}, u32[]{:S(2)}, u32[]{:S(2)}) collective-permute-start(bf16[2,2,64,256]{3,2,1,0:T(8,128)(2,1)S(1)} %constant_dynamic-update-slice_fusion.7.m0_ref), channel_id=1, source_target_pairs={{0,8},{1,9},{2,10},{3,11},{4,12},{5,13},{6,14},{7,15},{16,24},{17,... | collective-permute-start | bytes 393224 | tf_op jit(solution)/shard_map/ppermute | solution.py:50
  48.5 3.1 %collective-permute-start.18 = (bf16[2,512,256]{2,1,0:T(8,128)(2,1)S(1)}, bf16[2,512,256]{2,1,0:T(8,128)(2,1)S(1)}, u32[]{:S(2)}, u32[]{:S(2)}) collective-permute-start(bf16[2,512,256]{2,1,0:T(8,128)(2,1)S(1)} %get-tuple-element.21.kv_ref), channel_id=1, source_target_pairs={{0,2},{1,3},{2,4},{3,5},{4,6},{5,7},{6,8},{7,9},{8,10},{9,11},{10,... | collective-permute-start | bytes 1572872 | tf_op jit(solution)/shard_map/ppermute | solution.py:58
  51.8 2.7 %collective-permute-start.16 = (bf16[32,2,32,128]{3,2,1,0:T(8,128)(2,1)S(1)}, bf16[32,2,32,128]{3,2,1,0:T(8,128)(2,1)S(1)}, u32[]{:S(2)}, u32[]{:S(2)}) collective-permute-start(bf16[32,2,32,128]{3,2,1,0:T(8,128)(2,1)S(1)} %pad_maximum_fusion.1.refs_3_), channel_id=1, source_target_pairs={{0,12},{1,13},{2,14},{3,15},{4,0},{5,1},{6,2},{7,3},{8,4},{9,5},{1... | collective-permute-start | bytes 1572872 | tf_op jit(solution)/shard_map/ppermute | solution.py:50
  54.5 2.4 %collective-permute-start.15 = (bf16[32,2,32,128]{3,2,1,0:T(8,128)(2,1)S(1)}, bf16[32,2,32,128]{3,2,1,0:T(8,128)(2,1)S(1)}, u32[]{:S(2)}, u32[]{:S(2)}) collective-permute-start(bf16[32,2,32,128]{3,2,1,0:T(8,128)(2,1)S(1)} %pad_maximum_fusion.2.refs_4_), channel_id=1, source_target_pairs={{0,128},{1,129},{2,130},{3,131},{4,132},{5,133},{6,134},{7,135},{8... | collective-permute-start | bytes 1572872 | tf_op jit(solution)/shard_map/ppermute | solution.py:50
  56.9 1.5 %collective-permute-start.17 = (bf16[32,2,32,128]{3,2,1,0:T(8,128)(2,1)S(1)}, bf16[32,2,32,128]{3,2,1,0:T(8,128)(2,1)S(1)}, u32[]{:S(2)}, u32[]{:S(2)}) collective-permute-start(bf16[32,2,32,128]{3,2,1,0:T(8,128)(2,1)S(1)} %pad_maximum_fusion.2.refs_4_), channel_id=1, source_target_pairs={{0,130},{1,131},{2,128},{3,129},{4,134},{5,135},{6,132},{7,133},{8... | collective-permute-start | bytes 1572872 | tf_op jit(solution)/shard_map/ppermute | solution.py:50
  58.4 9.3 %far_0.1 = (f32[2,256,1024]{2,1,0:T(8,128)S(1)}, f32[2,256,128]{2,1,0:T(8,128)S(1)}) custom-call(s32[2]{0:T(128)S(1)} %pad_add_fusion.s_ref.refs_0_, bf16[256,2048]{1,0:T(8,128)(2,1)S(1)} %copy-done, bf16[256,1024]{1,0:T(8,128)(2,1)S(1)} %collective-permute-done.refs_2_.qb_ref, bf16[32,2,32,128]{3,2,1,0:T(8,128)(2,1)S(1)} %pad_maximum_fusion.1.refs_3_, ...), custom_call_target="tpu_custom_call" | custom-call | flops 3221225472 | bytes 6291456 | tf_op jit(solution)/shard_map/far_0/pallas_call | solution.py:252
  67.8 6.6 %near_own.1 = (f32[2,256,1024]{2,1,0:T(8,128)S(1)}, f32[2,256,128]{2,1,0:T(8,128)S(1)}) custom-call(s32[2]{0:T(128)S(1)} %pad_add_fusion.s_ref.refs_0_, bf16[256,2048]{1,0:T(8,128)(2,1)S(1)} %copy-done, bf16[256,1024]{1,0:T(8,128)(2,1)S(1)} %collective-permute-done.refs_2_.qb_ref, bf16[2,512,256]{2,1,0:T(8,128)(2,1)S(1)} %get-tuple-element.21.kv_ref), custom_call_target="tpu_custom_call" | custom-call | flops 1610612736 | bytes 6291456 | tf_op jit(solution)/shard_map/near_own/pallas_call | solution.py:252
  74.5 10.5 %near_mid.1.refs_8_ = f32[2,256,1024]{2,1,0:T(8,128)S(1)} custom-call(s32[2]{0:T(128)S(1)} %pad_add_fusion.s_ref.refs_0_, bf16[256,2048]{1,0:T(8,128)(2,1)S(1)} %copy-done, bf16[256,1024]{1,0:T(8,128)(2,1)S(1)} %collective-permute-done.refs_2_.qb_ref, bf16[2,512,256]{2,1,0:T(8,128)(2,1)S(1)} %collective-permute-done.18.kv_ref, ...), custom_call_target="tpu_custom_call" | custom-call | flops 3221225472 | bytes 6291456 | tf_op jit(solution)/shard_map/near_mid/pallas_call | solution.py:252
  85.0 1.8 %collective-permute-start.13 = (bf16[32,2,32,128]{3,2,1,0:T(8,128)(2,1)S(1)}, bf16[32,2,32,128]{3,2,1,0:T(8,128)(2,1)S(1)}, u32[]{:S(2)}, u32[]{:S(2)}) collective-permute-start(bf16[32,2,32,128]{3,2,1,0:T(8,128)(2,1)S(1)} %pad_maximum_fusion.2.refs_4_), channel_id=1, source_target_pairs={{0,2},{1,3},{2,0},{3,1},{4,6},{5,7},{6,4},{7,5},{8,10},{9,11},{10,... | collective-permute-start | bytes 1572872 | tf_op jit(solution)/shard_map/ppermute | solution.py:50
  86.9 14.9 %far_1.1 = (f32[2,256,1024]{2,1,0:T(8,128)S(1)}, f32[2,256,128]{2,1,0:T(8,128)S(1)}) custom-call(s32[2]{0:T(128)S(1)} %pad_add_fusion.s_ref.refs_0_, bf16[256,2048]{1,0:T(8,128)(2,1)S(1)} %copy-done, bf16[256,1024]{1,0:T(8,128)(2,1)S(1)} %collective-permute-done.refs_2_.qb_ref, bf16[32,2,32,128]{3,2,1,0:T(8,128)(2,1)S(1)} %collective-permute-done.14.refs_3_, ...), custom_call_target="tpu_custom_call" | custom-call | flops 6442450944 | bytes 6291456 | tf_op jit(solution)/shard_map/far_1/pallas_call | solution.py:252
  101.8 10.2 %far_2.1 = (bf16[256,1024]{1,0:T(8,128)(2,1)S(1)}, bf16[256,1024]{1,0:T(8,128)(2,1)S(1)}) custom-call(s32[2]{0:T(128)S(1)} %pad_add_fusion.s_ref.refs_0_, bf16[256,2048]{1,0:T(8,128)(2,1)S(1)} %copy-done, bf16[256,1024]{1,0:T(8,128)(2,1)S(1)} %collective-permute-done.refs_2_.qb_ref, bf16[32,2,32,128]{3,2,1,0:T(8,128)(2,1)S(1)} %collective-permute-done.9.refs_3_, ...), custom_call_target="tpu_custom_call" | custom-call | flops 3221225472 | bytes 6291456 | tf_op jit(solution)/shard_map/far_2/pallas_call | solution.py:252
  112.0 16.4 %collective-permute-start.23 = (bf16[256,1024]{1,0:T(8,128)(2,1)S(1)}, bf16[256,1024]{1,0:T(8,128)(2,1)S(1)}, u32[]{:S(2)}, u32[]{:S(2)}) collective-permute-start(bf16[256,1024]{1,0:T(8,128)(2,1)S(1)} %get-tuple-element.26), channel_id=1, source_target_pairs={{0,1},{1,0},{2,3},{3,2},{4,5},{5,4},{6,7},{7,6},{8,9},{9,8},{10,11... | collective-permute-start | bytes 1572872 | tf_op jit(solution)/shard_map/ppermute | solution.py:54
  128.4 1.5 %collective-permute-done.23 = bf16[256,1024]{1,0:T(8,128)(2,1)S(1)} collective-permute-done((bf16[256,1024]{1,0:T(8,128)(2,1)S(1)}, bf16[256,1024]{1,0:T(8,128)(2,1)S(1)}, u32[]{:S(2)}, u32[]{:S(2)}) %collective-permute-start.23) | collective-permute-done | bytes 524320 | tf_op jit(solution)/shard_map/ppermute | solution.py:54
  (79 shorter events, 11.6 us)
Async XLA Ops:
  1.5 55.4 %collective-permute-start = (bf16[256,1024]{1,0:T(8,128)(2,1)S(1)}, bf16[256,1024]{1,0:T(8,128)(2,1)S(1)}, u32[]{:S(2)}, u32[]{:S(2)}) collective-permute-start(bf16[256,1024]{1,0:T(8,128)(2,1)S(1)} %slice_select_fusion), channel_id=1, source_target_pairs={{0,1},{1,0},{2,3},{3,2},{4,5},{5,4},{6,7},{7,6},{8,9},{9,8},{10,11... | collective-permute-start | bytes 1572872 | tf_op jit(solution)/shard_map/ppermute | solution.py:54
  6.7 1.7 %collective-permute-start.1 = (bf16[2,256,256]{2,1,0:T(8,128)(2,1)}, bf16[2,256,256]{2,1,0:T(8,128)(2,1)S(1)}, u32[]{:S(2)}, u32[]{:S(2)}) collective-permute-start(bf16[2,256,256]{2,1,0:T(8,128)(2,1)} %pad_maximum_fusion.3), channel_id=1, source_target_pairs={{0,1},{1,0},{2,3},{3,2},{4,5},{5,4},{6,7},{7,6},{8,9},{9,8},{10,11... | collective-permute-start | bytes 786440 | tf_op jit(solution)/shard_map/ppermute | solution.py:54
  9.9 6.9 %collective-permute-start.2 = (bf16[2,1,2,32,128]{4,3,2,1,0:T(8,128)(2,1)S(1)}, bf16[2,1,2,32,128]{4,3,2,1,0:T(8,128)(2,1)S(1)}, u32[]{:S(2)}, u32[]{:S(2)}) collective-permute-start(bf16[2,1,2,32,128]{4,3,2,1,0:T(8,128)(2,1)S(1)} %get-tuple-element.16), channel_id=1, source_target_pairs={{0,64},{1,65},{2,66},{3,67},{4,68},{5,69},{6,70},{7,71},{8,72},{9,... | collective-permute-start | bytes 98312 | tf_op jit(solution)/shard_map/ppermute | solution.py:50
  16.8 6.8 %collective-permute-start.3 = (bf16[2,2,2,32,128]{4,3,2,1,0:T(8,128)(2,1)S(1)}, bf16[2,2,2,32,128]{4,3,2,1,0:T(8,128)(2,1)S(1)}, u32[]{:S(2)}, u32[]{:S(2)}) collective-permute-start(bf16[2,2,2,32,128]{4,3,2,1,0:T(8,128)(2,1)S(1)} %get-tuple-element.31), channel_id=1, source_target_pairs={{0,16},{1,17},{2,18},{3,19},{4,20},{5,21},{6,22},{7,23},{8,24},{9,... | collective-permute-start | bytes 196616 | tf_op jit(solution)/shard_map/ppermute | solution.py:50
  17.7 17.8 %collective-permute-start.19 = (bf16[1,2,64,256]{3,2,1,0:T(8,128)(2,1)S(1)}, bf16[1,2,64,256]{3,2,1,0:T(8,128)(2,1)S(1)}, u32[]{:S(2)}, u32[]{:S(2)}) collective-permute-start(bf16[1,2,64,256]{3,2,1,0:T(8,128)(2,1)S(1)} %get-tuple-element.22), channel_id=1, source_target_pairs={{0,2},{1,3},{2,0},{3,1},{4,6},{5,7},{6,4},{7,5},{8,10},{9,11},{10,... | collective-permute-start | bytes 196616 | tf_op jit(solution)/shard_map/ppermute | solution.py:50
  20.5 4.4 %collective-permute-start.4 = (bf16[2,2,2,32,128]{4,3,2,1,0:T(8,128)(2,1)S(1)}, bf16[2,2,2,32,128]{4,3,2,1,0:T(8,128)(2,1)S(1)}, u32[]{:S(2)}, u32[]{:S(2)}) collective-permute-start(bf16[2,2,2,32,128]{4,3,2,1,0:T(8,128)(2,1)S(1)} %get-tuple-element.31), channel_id=1, source_target_pairs={{0,112},{1,113},{2,114},{3,115},{4,116},{5,117},{6,118},{7,119},{8... | collective-permute-start | bytes 196616 | tf_op jit(solution)/shard_map/ppermute | solution.py:50
  23.5 5.9 %collective-permute-start.5 = (bf16[2,2,2,32,128]{4,3,2,1,0:T(8,128)(2,1)S(1)}, bf16[2,2,2,32,128]{4,3,2,1,0:T(8,128)(2,1)S(1)}, u32[]{:S(2)}, u32[]{:S(2)}) collective-permute-start(bf16[2,2,2,32,128]{4,3,2,1,0:T(8,128)(2,1)S(1)} %get-tuple-element.31), channel_id=1, source_target_pairs={{0,32},{1,33},{2,34},{3,35},{4,36},{5,37},{6,38},{7,39},{8,40},{9,... | collective-permute-start | bytes 196616 | tf_op jit(solution)/shard_map/ppermute | solution.py:50
  29.4 9.1 %collective-permute-start.8 = (bf16[8,2,32,128]{3,2,1,0:T(8,128)(2,1)S(1)}, bf16[8,2,32,128]{3,2,1,0:T(8,128)(2,1)S(1)}, u32[]{:S(2)}, u32[]{:S(2)}) collective-permute-start(bf16[8,2,32,128]{3,2,1,0:T(8,128)(2,1)S(1)} %get-tuple-element.30), channel_id=1, source_target_pairs={{0,2},{1,3},{2,0},{3,1},{4,6},{5,7},{6,4},{7,5},{8,10},{9,11},{10,... | collective-permute-start | bytes 393224 | tf_op jit(solution)/shard_map/ppermute | solution.py:50
  29.5 9.8 %collective-permute-start.7 = (bf16[8,2,32,128]{3,2,1,0:T(8,128)(2,1)S(1)}, bf16[8,2,32,128]{3,2,1,0:T(8,128)(2,1)S(1)}, u32[]{:S(2)}, u32[]{:S(2)}) collective-permute-start(bf16[8,2,32,128]{3,2,1,0:T(8,128)(2,1)S(1)} %get-tuple-element.30), channel_id=1, source_target_pairs={{0,130},{1,131},{2,128},{3,129},{4,134},{5,135},{6,132},{7,133},{8... | collective-permute-start | bytes 393224 | tf_op jit(solution)/shard_map/ppermute | solution.py:50
  34.2 5.9 %collective-permute-start.6 = (bf16[8,2,32,128]{3,2,1,0:T(8,128)(2,1)S(1)}, bf16[8,2,32,128]{3,2,1,0:T(8,128)(2,1)S(1)}, u32[]{:S(2)}, u32[]{:S(2)}) collective-permute-start(bf16[8,2,32,128]{3,2,1,0:T(8,128)(2,1)S(1)} %get-tuple-element.30), channel_id=1, source_target_pairs={{0,128},{1,129},{2,130},{3,131},{4,132},{5,133},{6,134},{7,135},{8... | collective-permute-start | bytes 393224 | tf_op jit(solution)/shard_map/ppermute | solution.py:50
  35.5 6.9 %collective-permute-start.12 = (bf16[8,2,32,128]{3,2,1,0:T(8,128)(2,1)S(1)}, bf16[8,2,32,128]{3,2,1,0:T(8,128)(2,1)S(1)}, u32[]{:S(2)}, u32[]{:S(2)}) collective-permute-start(bf16[8,2,32,128]{3,2,1,0:T(8,128)(2,1)S(1)} %get-tuple-element.29), channel_id=1, source_target_pairs={{0,8},{1,9},{2,10},{3,11},{4,12},{5,13},{6,14},{7,15},{8,0},{9,1},... | collective-permute-start | bytes 393224 | tf_op jit(solution)/shard_map/ppermute | solution.py:50
  38.5 8.6 %collective-permute-start.11 = (bf16[8,2,32,128]{3,2,1,0:T(8,128)(2,1)S(1)}, bf16[8,2,32,128]{3,2,1,0:T(8,128)(2,1)S(1)}, u32[]{:S(2)}, u32[]{:S(2)}) collective-permute-start(bf16[8,2,32,128]{3,2,1,0:T(8,128)(2,1)S(1)} %get-tuple-element.29), channel_id=1, source_target_pairs={{0,12},{1,13},{2,14},{3,15},{4,0},{5,1},{6,2},{7,3},{8,4},{9,5},{1... | collective-permute-start | bytes 393224 | tf_op jit(solution)/shard_map/ppermute | solution.py:50
  39.3 9.2 %collective-permute-start.10 = (bf16[8,2,32,128]{3,2,1,0:T(8,128)(2,1)S(1)}, bf16[8,2,32,128]{3,2,1,0:T(8,128)(2,1)S(1)}, u32[]{:S(2)}, u32[]{:S(2)}) collective-permute-start(bf16[8,2,32,128]{3,2,1,0:T(8,128)(2,1)S(1)} %get-tuple-element.29), channel_id=1, source_target_pairs={{0,4},{1,5},{2,6},{3,7},{4,8},{5,9},{6,10},{7,11},{8,12},{9,13},{1... | collective-permute-start | bytes 393224 | tf_op jit(solution)/shard_map/ppermute | solution.py:50
  40.1 11.6 %collective-permute-start.20 = (bf16[2,2,64,256]{3,2,1,0:T(8,128)(2,1)S(1)}, bf16[2,2,64,256]{3,2,1,0:T(8,128)(2,1)S(1)}, u32[]{:S(2)}, u32[]{:S(2)}) collective-permute-start(bf16[2,2,64,256]{3,2,1,0:T(8,128)(2,1)S(1)} %constant_dynamic-update-slice_fusion.7.m0_ref), channel_id=1, source_target_pairs={{0,4},{1,5},{2,6},{3,7},{4,8},{5,9},{6,10},{7,11},{8,12},{9,13},{1... | collective-permute-start | bytes 393224 | tf_op jit(solution)/shard_map/ppermute | solution.py:50
  42.4 9.4 %collective-permute-start.21 = (bf16[2,2,64,256]{3,2,1,0:T(8,128)(2,1)S(1)}, bf16[2,2,64,256]{3,2,1,0:T(8,128)(2,1)S(1)}, u32[]{:S(2)}, u32[]{:S(2)}) collective-permute-start(bf16[2,2,64,256]{3,2,1,0:T(8,128)(2,1)S(1)} %constant_dynamic-update-slice_fusion.7.m0_ref), channel_id=1, source_target_pairs={{0,8},{1,9},{2,10},{3,11},{4,12},{5,13},{6,14},{7,15},{16,24},{17,... | collective-permute-start | bytes 393224 | tf_op jit(solution)/shard_map/ppermute | solution.py:50
  47.1 7.4 %collective-permute-start.22 = (bf16[2,2,64,256]{3,2,1,0:T(8,128)(2,1)S(1)}, bf16[2,2,64,256]{3,2,1,0:T(8,128)(2,1)S(1)}, u32[]{:S(2)}, u32[]{:S(2)}) collective-permute-start(bf16[2,2,64,256]{3,2,1,0:T(8,128)(2,1)S(1)} %constant_dynamic-update-slice_fusion.7.m0_ref), channel_id=1, source_target_pairs={{0,12},{1,13},{2,14},{3,15},{16,28},{17,29},{18,30},{19,31},{32,44... | collective-permute-start | bytes 393224 | tf_op jit(solution)/shard_map/ppermute | solution.py:50
  48.5 25.9 %collective-permute-start.18 = (bf16[2,512,256]{2,1,0:T(8,128)(2,1)S(1)}, bf16[2,512,256]{2,1,0:T(8,128)(2,1)S(1)}, u32[]{:S(2)}, u32[]{:S(2)}) collective-permute-start(bf16[2,512,256]{2,1,0:T(8,128)(2,1)S(1)} %get-tuple-element.21.kv_ref), channel_id=1, source_target_pairs={{0,2},{1,3},{2,4},{3,5},{4,6},{5,7},{6,8},{7,9},{8,10},{9,11},{10,... | collective-permute-start | bytes 1572872 | tf_op jit(solution)/shard_map/ppermute | solution.py:58
  51.7 33.3 %collective-permute-start.14 = (bf16[32,2,32,128]{3,2,1,0:T(8,128)(2,1)S(1)}, bf16[32,2,32,128]{3,2,1,0:T(8,128)(2,1)S(1)}, u32[]{:S(2)}, u32[]{:S(2)}) collective-permute-start(bf16[32,2,32,128]{3,2,1,0:T(8,128)(2,1)S(1)} %pad_maximum_fusion.1.refs_3_), channel_id=1, source_target_pairs={{0,4},{1,5},{2,6},{3,7},{4,8},{5,9},{6,10},{7,11},{8,12},{9,13},{1... | collective-permute-start | bytes 1572872 | tf_op jit(solution)/shard_map/ppermute | solution.py:50
  51.8 35.0 %collective-permute-start.16 = (bf16[32,2,32,128]{3,2,1,0:T(8,128)(2,1)S(1)}, bf16[32,2,32,128]{3,2,1,0:T(8,128)(2,1)S(1)}, u32[]{:S(2)}, u32[]{:S(2)}) collective-permute-start(bf16[32,2,32,128]{3,2,1,0:T(8,128)(2,1)S(1)} %pad_maximum_fusion.1.refs_3_), channel_id=1, source_target_pairs={{0,12},{1,13},{2,14},{3,15},{4,0},{5,1},{6,2},{7,3},{8,4},{9,5},{1... | collective-permute-start | bytes 1572872 | tf_op jit(solution)/shard_map/ppermute | solution.py:50
  54.5 32.4 %collective-permute-start.15 = (bf16[32,2,32,128]{3,2,1,0:T(8,128)(2,1)S(1)}, bf16[32,2,32,128]{3,2,1,0:T(8,128)(2,1)S(1)}, u32[]{:S(2)}, u32[]{:S(2)}) collective-permute-start(bf16[32,2,32,128]{3,2,1,0:T(8,128)(2,1)S(1)} %pad_maximum_fusion.2.refs_4_), channel_id=1, source_target_pairs={{0,128},{1,129},{2,130},{3,131},{4,132},{5,133},{6,134},{7,135},{8... | collective-permute-start | bytes 1572872 | tf_op jit(solution)/shard_map/ppermute | solution.py:50
  56.9 29.9 %collective-permute-start.17 = (bf16[32,2,32,128]{3,2,1,0:T(8,128)(2,1)S(1)}, bf16[32,2,32,128]{3,2,1,0:T(8,128)(2,1)S(1)}, u32[]{:S(2)}, u32[]{:S(2)}) collective-permute-start(bf16[32,2,32,128]{3,2,1,0:T(8,128)(2,1)S(1)} %pad_maximum_fusion.2.refs_4_), channel_id=1, source_target_pairs={{0,130},{1,131},{2,128},{3,129},{4,134},{5,135},{6,132},{7,133},{8... | collective-permute-start | bytes 1572872 | tf_op jit(solution)/shard_map/ppermute | solution.py:50
  74.4 27.4 %collective-permute-start.9 = (bf16[32,2,32,128]{3,2,1,0:T(8,128)(2,1)S(1)}, bf16[32,2,32,128]{3,2,1,0:T(8,128)(2,1)S(1)}, u32[]{:S(2)}, u32[]{:S(2)}) collective-permute-start(bf16[32,2,32,128]{3,2,1,0:T(8,128)(2,1)S(1)} %pad_maximum_fusion.1.refs_3_), channel_id=1, source_target_pairs={{0,8},{1,9},{2,10},{3,11},{4,12},{5,13},{6,14},{7,15},{8,0},{9,1},... | collective-permute-start | bytes 1572872 | tf_op jit(solution)/shard_map/ppermute | solution.py:50
  85.0 16.8 %collective-permute-start.13 = (bf16[32,2,32,128]{3,2,1,0:T(8,128)(2,1)S(1)}, bf16[32,2,32,128]{3,2,1,0:T(8,128)(2,1)S(1)}, u32[]{:S(2)}, u32[]{:S(2)}) collective-permute-start(bf16[32,2,32,128]{3,2,1,0:T(8,128)(2,1)S(1)} %pad_maximum_fusion.2.refs_4_), channel_id=1, source_target_pairs={{0,2},{1,3},{2,0},{3,1},{4,6},{5,7},{6,4},{7,5},{8,10},{9,11},{10,... | collective-permute-start | bytes 1572872 | tf_op jit(solution)/shard_map/ppermute | solution.py:50
  112.0 17.9 %collective-permute-start.23 = (bf16[256,1024]{1,0:T(8,128)(2,1)S(1)}, bf16[256,1024]{1,0:T(8,128)(2,1)S(1)}, u32[]{:S(2)}, u32[]{:S(2)}) collective-permute-start(bf16[256,1024]{1,0:T(8,128)(2,1)S(1)} %get-tuple-element.26), channel_id=1, source_target_pairs={{0,1},{1,0},{2,3},{3,2},{4,5},{5,4},{6,7},{7,6},{8,9},{9,8},{10,11... | collective-permute-start | bytes 1572872 | tf_op jit(solution)/shard_map/ppermute | solution.py:54
  (13 other events, 139.6 us)
